TPU v7x, 32 devices: a whole 2x2x4 slice. The times are simulated.
32 devices in a mesh: outer: 1, inner: 32 (over z, y, x, core).
Axes of the slice: x: 2, y: 2, z: 4, core: 2. Of those that a mesh axis runs over, the one named last changes fastest.
Arguments:
- b_leaf: float32 [8192, 64], P(('outer', 'inner')), may hold values from -6 to 6
- b_sep: float32 [256, 64], P(('outer', 'inner')), may hold values from -6 to 6
- b_root: float32 [256, 64], P(('outer', 'inner')), may hold values from -6 to 6
- leaf_linv: float32 [8192, 256], P(('outer', 'inner')), as said below
- leaf_uinv: float32 [8192, 256], P(('outer', 'inner')), as said below
- leaf_lower: float32 [8192, 256], P(('outer', 'inner')), as said below
- leaf_upper: float32 [8192, 256], P(('outer', 'inner')), as said below
- sep_rows: int32 [32, 256], P(('outer', 'inner')), may hold values from 0 to 255, as said below
- sep_linv: float32 [256, 256], P(('outer', 'inner')), as said below
- sep_uinv: float32 [256, 256], P(('outer', 'inner')), as said below
- sep_lower: float32 [256, 256], P(None, ('outer', 'inner')), as said below
- sep_upper: float32 [256, 256], P(('outer', 'inner')), as said below
- root_linv: float32 [256, 256], P(('outer', 'inner')), as said below
- root_uinv: float32 [256, 256], P(('outer', 'inner')), as said below
- basis_leaf: float32 [8192, 512], P(('outer', 'inner')), as said below
- basis_sep: float32 [256, 512], P(('outer', 'inner')), as said below
- basis_root: float32 [256, 512], P(('outer', 'inner')), as said below
- g_blocks: float32 [32768, 128], P(('outer', 'inner')), may hold values from -0.25 to 0.25
- c_blocks: float32 [32768, 128], P(('outer', 'inner')), may hold values from -0.25 to 0.25
- block_cols: int32 [64, 4], P(('outer', 'inner')), may hold values from 0 to 1
Outputs:
- v_leaf: float32 [8192, 64], P(('outer', 'inner'))
- v_sep: float32 [256, 64], P(('outer', 'inner'))
- v_root: float32 [256, 64], P(('outer', 'inner'))
- coefficients: float32 [512, 64], replicated
- reduced_g: float32 [64, 64], replicated
- reduced_c: float32 [64, 64], replicated
Inputs may be any that keep to these rules, and one draw needn't show every extreme that they name: `sep_rows`: each row holds 256 distinct numbers; every row names 0 and 255. `leaf_linv`: lower triangular in each diagonal block of the stack, nonzero diagonal. `leaf_uinv`: upper triangular in each diagonal block of the stack, nonzero diagonal. `sep_linv`: lower triangular in each block of 256 rows, nonzero diagonal. `sep_uinv`: upper triangular in each block of 256 rows, nonzero diagonal. `root_linv`: lower triangular, nonzero diagonal. `root_uinv`: upper triangular, nonzero diagonal. `leaf_lower`: entries of order one over the square root of 256. `leaf_upper`: entries of order one over the square root of 256. `sep_lower`: entries of order one over the square root of the number of its columns. `sep_upper`: entries of order one over the square root of 256. basis_leaf, basis_sep and basis_root stacked by rows form Q with Q^T Q = 8704 I up to float32 rounding. `basis_sep`: part of the stacked Q described with basis_leaf. `basis_root`: part of the stacked Q described with basis_leaf.
All inputs are finite; a program needn't handle non-finite values.
Results may differ from a plain program's by a relative error of at most 0.0003.
Values sent between devices are 32-bit elements; how exact they have to be, the bound alone decides.
No kernel may reach another device: no remote copies, remote signals or barrier semaphores. Data moves between devices by JAX's collectives and lax.ppermute only.
A program may use at most 64 MiB of HBM per device.

v0:
```python
import jax
import jax.numpy as jnp
from jax import lax
from jax.sharding import PartitionSpec as P


def matmul_exact(left, right):
    return jnp.dot(left, right, precision=lax.Precision.HIGHEST, preferred_element_type=jnp.float32)


def contract_rows(left, right):
    return lax.dot_general(
        left,
        right,
        (((0,), (0,)), ((), ())),
        precision=lax.Precision.HIGHEST,
        preferred_element_type=jnp.float32,
    )


def shards(
    b_leaf,
    b_sep,
    b_root,
    leaf_linv,
    leaf_uinv,
    leaf_lower,
    leaf_upper,
    sep_rows,
    sep_linv,
    sep_uinv,
    sep_lower,
    sep_upper,
    root_linv,
    root_uinv,
    basis_leaf,
    basis_sep,
    basis_root,
    g_blocks,
    c_blocks,
    block_cols,
):
    ports = b_leaf.shape[1]
    sep_local = b_sep.shape[0]
    root_local = b_root.shape[0]
    sep_width = sep_linv.shape[1]
    selector = (sep_rows[0][:, None] == jnp.arange(sep_width, dtype=jnp.int32)[None, :]).astype(
        jnp.float32
    )
    y_leaf = matmul_exact(leaf_linv, b_leaf)
    contrib = matmul_exact(leaf_lower, y_leaf)
    t_sep = lax.psum_scatter(
        contract_rows(selector, contrib), "inner", scatter_dimension=0, tiled=True
    )
    sep_whole = lax.all_gather(b_sep - t_sep, "inner", axis=0, tiled=True)
    y_sep = matmul_exact(sep_linv, sep_whole)
    summed = lax.psum(matmul_exact(sep_lower, y_sep), ("outer", "inner"))
    sources = lax.all_gather(b_root, ("outer", "inner"), axis=0, tiled=True)
    y_root = matmul_exact(root_linv, sources - summed)
    y_root_all = lax.all_gather(y_root, ("outer", "inner"), axis=0, tiled=True)
    x_root = matmul_exact(root_uinv, y_root_all)
    x_root_all = lax.all_gather(x_root, ("outer", "inner"), axis=0, tiled=True)
    z_sep = y_sep - matmul_exact(sep_upper, x_root_all)
    z_sep_all = lax.all_gather(z_sep, "inner", axis=0, tiled=True)
    x_sep = matmul_exact(sep_uinv, z_sep_all)
    x_sep_all = lax.all_gather(x_sep, "inner", axis=0, tiled=True)
    coupled = matmul_exact(selector, x_sep_all)
    x_leaf = matmul_exact(leaf_uinv, y_leaf - matmul_exact(leaf_upper, coupled))
    node_count = float(
        lax.axis_size("outer") * lax.axis_size("inner") * (b_leaf.shape[0] + sep_local + root_local)
    )
    pieces_x = (x_leaf, x_sep, x_root)
    pieces_q = (basis_leaf, basis_sep, basis_root)
    projected = (
        contract_rows(basis_leaf, x_leaf)
        + contract_rows(basis_sep, x_sep)
        + contract_rows(basis_root, x_root)
    )
    coefficients = lax.psum(projected, ("outer", "inner")) / node_count
    cleaned = [
        values - matmul_exact(basis, coefficients) for basis, values in zip(pieces_q, pieces_x)
    ]
    local_gram = (
        contract_rows(cleaned[0], cleaned[0])
        + contract_rows(cleaned[1], cleaned[1])
        + contract_rows(cleaned[2], cleaned[2])
    )
    gram_matrix = lax.psum(local_gram, ("outer", "inner")) / node_count
    chol_lower = jnp.linalg.cholesky(gram_matrix)
    inverse_lower = lax.linalg.triangular_solve(
        chol_lower, jnp.eye(ports, dtype=jnp.float32), left_side=True, lower=True
    )
    v_leaf = matmul_exact(cleaned[0], inverse_lower.T)
    v_sep = matmul_exact(cleaned[1], inverse_lower.T)
    v_root = matmul_exact(cleaned[2], inverse_lower.T)
    block_rows = block_cols.shape[0]
    stored = block_cols.shape[1]
    block_size = g_blocks.shape[1]
    blocked = v_leaf.reshape(block_rows, block_size, ports)
    picked = blocked[block_cols]
    g_tiles = g_blocks.reshape(block_rows, stored, block_size, block_size)
    c_tiles = c_blocks.reshape(block_rows, stored, block_size, block_size)
    g_image = jnp.einsum("rwij,rwjp->rip", g_tiles, picked, precision=lax.Precision.HIGHEST)
    c_image = jnp.einsum("rwij,rwjp->rip", c_tiles, picked, precision=lax.Precision.HIGHEST)
    g_local = jnp.einsum("rip,riq->pq", blocked, g_image, precision=lax.Precision.HIGHEST)
    c_local = jnp.einsum("rip,riq->pq", blocked, c_image, precision=lax.Precision.HIGHEST)
    g_summed, c_summed = lax.psum((g_local, c_local), ("outer", "inner"))
    return (v_leaf, v_sep, v_root, coefficients, g_summed / node_count, c_summed / node_count)


def solution(mesh):
    return jax.shard_map(
        shards,
        mesh=mesh,
        in_specs=(
            P(("outer", "inner"), None),
            P(("outer", "inner"), None),
            P(("outer", "inner"), None),
            P(("outer", "inner"), None),
            P(("outer", "inner"), None),
            P(("outer", "inner"), None),
            P(("outer", "inner"), None),
            P(("outer", "inner"), None),
            P(("outer", "inner"), None),
            P(("outer", "inner"), None),
            P(None, ("outer", "inner")),
            P(("outer", "inner"), None),
            P(("outer", "inner"), None),
            P(("outer", "inner"), None),
            P(("outer", "inner"), None),
            P(("outer", "inner"), None),
            P(("outer", "inner"), None),
            P(("outer", "inner"), None),
            P(("outer", "inner"), None),
            P(("outer", "inner"), None),
        ),
        out_specs=(
            P(("outer", "inner"), None),
            P(("outer", "inner"), None),
            P(("outer", "inner"), None),
            P(),
            P(),
            P(),
        ),
        check_vma=False,
    )
```

profile of v0, /device:TPU:0, one launch (start us, length us, event | category | flops | bytes accessed | tf_op | source)
XLA Modules:
  0.0 685.7 jit_solution(16916968704119471954)
XLA Ops:
  7.2 1.4 fusion.17
  8.6 0.4 fusion.18
  9.0 0.7 copy-done.16
  9.7 1.0 fusion.8
  10.8 130.4 %all-reduce.10.cloned.1.call-done = f32[256,64]{1,0:T(8,128)} async-done(((f32[256,64]{1,0:T(8,128)}), f32[256,64]{1,0:T(8,128)}) %all-reduce.10.cloned.1.call-update) | async-done | bytes 65552
  141.3 0.7 dynamic-slice_subtract_fusion
  142.0 40.0 %all_gather.18 = f32[256,64]{1,0:T(8,128)S(1)} all-gather(f32[8,64]{1,0:T(8,128)S(1)} %dynamic-slice_subtract_fusion), channel_id=1, replica_groups=mesh['outer'=1,'inner'=32] {'inner'}, dimensions={0}, use_global_device_ids=true | all-gather | bytes 67584 | tf_op jit(solution)/shard_map/all_gather | solution.py:55
  182.2 0.5 copy-done.11
  182.7 0.9 convolution_bitcast_fusion.3
  183.7 0.6 copy-done.19
  184.3 37.0 %all_gather.19 = f32[256,64]{1,0:T(8,128)S(1)} all-gather(f32[8,64]{1,0:T(8,128)S(1)} %copy-done.18), channel_id=1, replica_groups=mesh['outer'=1,'inner'=32] {'outer','inner'}, dimensions={0}, use_global_device_ids=true | all-gather | bytes 67584 | tf_op jit(solution)/shard_map/all_gather | solution.py:58
  221.4 77.8 %all-reduce.6.cloned.1.call-done = f32[256,64]{0,1:T(8,128)} async-done(((f32[256,64]{0,1:T(8,128)}), f32[256,64]{0,1:T(8,128)}) %all-reduce.6.cloned.1.call-update) | async-done | bytes 65552 | tf_op jit(solution)/shard_map/psum | solution.py:57
  299.2 1.0 convolution_bitcast_fusion.8
  300.2 40.4 %all_gather.20 = f32[256,64]{1,0:T(8,128)S(1)} all-gather(f32[8,64]{1,0:T(8,128)S(1)} %convolution_bitcast_fusion.8), channel_id=1, replica_groups=mesh['outer'=1,'inner'=32] {'outer','inner'}, dimensions={0}, use_global_device_ids=true | all-gather | bytes 67584 | tf_op jit(solution)/shard_map/all_gather | solution.py:60
  340.8 37.0 %all_gather.21 = f32[256,64]{1,0:T(8,128)S(1)} all-gather(f32[8,64]{1,0:T(8,128)S(1)} %bitcast.119), channel_id=1, replica_groups=mesh['outer'=1,'inner'=32] {'outer','inner'}, dimensions={0}, use_global_device_ids=true | all-gather | bytes 67584 | tf_op jit(solution)/shard_map/all_gather | solution.py:62
  377.9 38.3 %all_gather.22 = f32[256,64]{1,0:T(8,128)S(1)} all-gather(f32[8,64]{1,0:T(8,128)S(1)} %fusion.5), channel_id=1, replica_groups=mesh['outer'=1,'inner'=32] {'inner'}, dimensions={0}, use_global_device_ids=true | all-gather | bytes 67584 | tf_op jit(solution)/shard_map/all_gather | solution.py:64
  416.4 37.0 %all_gather.23 = f32[256,64]{1,0:T(8,128)S(1)} all-gather(f32[8,64]{1,0:T(8,128)S(1)} %bitcast.120), channel_id=1, replica_groups=mesh['outer'=1,'inner'=32] {'inner'}, dimensions={0}, use_global_device_ids=true | all-gather | bytes 67584 | tf_op jit(solution)/shard_map/all_gather | solution.py:66
  453.4 0.3 fusion.6
  453.8 0.3 fusion.24
  454.2 0.3 fusion.23
  454.5 0.4 fusion.2
  454.9 0.4 fusion.22
  455.2 1.1 fusion.1
  456.4 122.1 %all-reduce.8.cloned.1.call-done = f32[512,64]{0,1:T(8,128)} async-done(((f32[512,64]{0,1:T(8,128)}), f32[512,64]{0,1:T(8,128)}) %all-reduce.8.cloned.1.call-update) | async-done | bytes 131088 | tf_op jit(solution)/shard_map/psum | solution.py:79
  578.5 0.9 broadcast_multiply_fusion
  579.4 0.6 convolution_subtract_fusion
  580.0 0.2 fusion.4
  580.2 0.2 fusion.3
  580.4 0.2 fusion.25
  580.7 0.2 convolution_add_fusion.2
  580.9 0.2 convolution_add_fusion.1
  581.2 39.4 %psum.37 = f32[64,64]{0,1:T(8,128)S(1)} all-reduce(f32[64,64]{0,1:T(8,128)S(1)} %convolution_add_fusion.1), channel_id=1, replica_groups=mesh['outer'=1,'inner'=32] {'outer','inner'}, use_global_device_ids=true, to_apply=%region_3.0 | all-reduce | flops 4096 | bytes 32768 | tf_op jit(solution)/shard_map/psum | solution.py:88
  620.7 5.8 cholesky.17
  626.6 0.6 compare_reduce_fusion
  627.2 0.7 fusion.13
  627.9 4.9 custom-call.6
  632.8 0.2 fusion.14
  633.0 0.2 fusion.26
  633.3 0.8 fusion.27
  634.0 0.8 fusion.28
  634.8 0.6 gather_fusion
  635.4 0.7 convolution_bitcast_fusion.1
  636.0 0.2 convolution_bitcast_fusion.5
  636.4 0.7 convolution_bitcast_fusion
  637.1 0.2 convolution_bitcast_fusion.4
  637.3 40.4 %all-reduce.1 = (f32[64,64]{0,1:T(8,128)S(1)}, f32[64,64]{0,1:T(8,128)S(1)}) all-reduce(f32[64,64]{0,1:T(8,128)S(1)} %convolution_bitcast_fusion.5, f32[64,64]{0,1:T(8,128)S(1)} %convolution_bitcast_fusion.4), channel_id=1, replica_groups=mesh['outer'=1,'inner'=32] {'outer','inner'}, use_global_device_ids=true, to_apply=%region_6.7 | all-reduce | flops 8192 | bytes 65536 | tf_op jit(solution)/shard_map/psum | solution.py:107
  677.7 0.7 copy.69
  678.4 0.7 copy.70
  (57 shorter events, 1.5 us)
Async XLA Ops:
  7.2 628.2 %copy-start = (f32[1024,128]{1,0:T(8,128)S(1)}, f32[1024,128]{1,0:T(8,128)}, u32[]{:S(2)}) copy-start(f32[1024,128]{1,0:T(8,128)} %param.37) | copy-start | bytes 1572868
  7.2 1.5 copy-start.6
  7.2 134.1 %all-reduce.10.cloned.1.call-start = ((), (), s32[]{:S(2)}) async-start(), calls=%async_computation.2 | async-start | bytes 262144
  9.0 0.7 copy-start.16
  10.8 288.5 %all-reduce.6.cloned.1.call-start = ((), (), s32[]{:S(2)}) async-start(), calls=%async_computation | async-start | bytes 131072 | tf_op jit(solution)/shard_map/psum | solution.py:57
  10.8 130.5 %copy-start.17 = (f32[8,64]{1,0:T(8,128)S(1)}, f32[8,64]{1,0:T(8,128)}, u32[]{:S(2)}) copy-start(f32[8,64]{1,0:T(8,128)} %param.21) | copy-start | bytes 6148
  142.0 40.0 %copy-start.10 = (f32[8,256]{1,0:T(8,128)S(1)}, f32[8,256]{1,0:T(8,128)}, u32[]{:S(2)}) copy-start(f32[8,256]{1,0:T(8,128)} %param.28) | copy-start | bytes 24580
  182.0 0.7 copy-start.11
  183.6 0.7 copy-start.19
  183.6 0.7 copy-start.18
  183.6 394.9 %all-reduce.8.cloned.1.call-start = ((), (), s32[]{:S(2)}) async-start(), calls=%async_computation.1 | async-start | bytes 262144 | tf_op jit(solution)/shard_map/psum | solution.py:79
  221.3 78.0 %copy-start.12 = (f32[8,256]{1,0:T(8,128)S(1)}, f32[8,256]{1,0:T(8,128)}, u32[]{:S(2)}) copy-start(f32[8,256]{1,0:T(8,128)} %param.32) | copy-start | bytes 24580
  300.2 40.4 %copy-start.13 = (f32[8,256]{1,0:T(8,128)S(1)}, f32[8,256]{1,0:T(8,128)}, u32[]{:S(2)}) copy-start(f32[8,256]{1,0:T(8,128)} %param.33) | copy-start | bytes 24580
  340.8 37.0 %copy-start.14 = (f32[8,256]{1,0:T(8,128)S(1)}, f32[8,256]{1,0:T(8,128)}, u32[]{:S(2)}) copy-start(f32[8,256]{1,0:T(8,128)} %param.31) | copy-start | bytes 24580
  377.9 38.3 %copy-start.15 = (f32[8,256]{1,0:T(8,128)S(1)}, f32[8,256]{1,0:T(8,128)}, u32[]{:S(2)}) copy-start(f32[8,256]{1,0:T(8,128)} %param.29) | copy-start | bytes 24580
  416.4 37.3 %copy-start.9 = (f32[8,512]{1,0:T(8,128)S(1)}, f32[8,512]{1,0:T(8,128)}, u32[]{:S(2)}) copy-start(f32[8,512]{1,0:T(8,128)} %param.36) | copy-start | bytes 49156
  453.4 0.7 copy-start.8
  453.4 1.0 copy-start.5
  453.8 1.1 copy-start.7
  454.1 1.1 copy-start.1
  579.4 0.8 copy-start.2
  633.2 3.8 copy-start.3
  635.4 1.0 copy-start.4
Sparse Core Ops, SparseCore 0:
  14.1 127.1 all-reduce.9
  183.7 115.4 all-reduce.5
  456.5 121.9 all-reduce.7
where the time goes:
time: 686 us
  waiting for transfers between devices  330 us (48%)
  blocking collectives  309 us (45%)
  between operations  14.1 us (2%)
  other arithmetic  13.7 us (2%)
  matrix products  13.6 us (2%)
    unnamed x4, waiting for transfers between devices  130 us
    psum x1, waiting for transfers between devices, shards(): coefficients = lax.psum(projected, ('outer', 'inner')) / node_count  122 us
    psum x1, waiting for transfers between devices, shards(): summed = lax.psum(matmul_exact(sep_lower, y_sep), ('outer', 'inner'))  77.8 us
    psum x1, blocking collectives, shards(): g_summed, c_summed = lax.psum((g_local, c_local), ('outer', 'inner'))  40.4 us
    all_gather x1, blocking collectives, shards(): y_root_all = lax.all_gather(y_root, ('outer', 'inner'), axis=0, tiled=True)  40.4 us
    all_gather x1, blocking collectives, shards(): sep_whole = lax.all_gather(b_sep - t_sep, 'inner', axis=0, tiled=True)  40 us
    psum x1, blocking collectives, shards(): gram_matrix = lax.psum(local_gram, ('outer', 'inner')) / node_count  39.4 us
    all_gather x1, blocking collectives, shards(): z_sep_all = lax.all_gather(z_sep, 'inner', axis=0, tiled=True)  38.3 us
  transfers between devices with their start and end apart: 3, of which 3 were waited for; matrix products, arithmetic and copies ran while one was open for 0% of the time, Pallas kernels for 0%

commit v1 on v0

--- a/solution.py
+++ b/solution.py
@@ -54,7 +54,7 @@
     )
     sep_whole = lax.all_gather(b_sep - t_sep, "inner", axis=0, tiled=True)
     y_sep = matmul_exact(sep_linv, sep_whole)
-    summed = lax.psum(matmul_exact(sep_lower, y_sep), ("outer", "inner"))
+    summed = lax.psum(lax.psum(matmul_exact(sep_lower, y_sep), "outer"), "inner")
     sources = lax.all_gather(b_root, ("outer", "inner"), axis=0, tiled=True)
     y_root = matmul_exact(root_linv, sources - summed)
     y_root_all = lax.all_gather(y_root, ("outer", "inner"), axis=0, tiled=True)

time: 686 us -> 686 us (level)
  no operation moved by 1% of the time
where the time goes in v1:
time: 686 us
  waiting for transfers between devices  330 us (48%)
  blocking collectives  309 us (45%)
  between operations  14.1 us (2%)
  other arithmetic  13.7 us (2%)
  matrix products  13.6 us (2%)
    unnamed x4, waiting for transfers between devices  130 us
    psum x1, waiting for transfers between devices, shards(): coefficients = lax.psum(projected, ('outer', 'inner')) / node_count  122 us
    psum x1, waiting for transfers between devices, shards(): lax.psum(lax.psum(matmul_exact(sep_lower, y_sep), 'outer'), 'inner')  77.8 us
    psum x1, blocking collectives, shards(): g_summed, c_summed = lax.psum((g_local, c_local), ('outer', 'inner'))  40.4 us
    all_gather x1, blocking collectives, shards(): y_root_all = lax.all_gather(y_root, ('outer', 'inner'), axis=0, tiled=True)  40.4 us
    all_gather x1, blocking collectives, shards(): sep_whole = lax.all_gather(b_sep - t_sep, 'inner', axis=0, tiled=True)  40 us
    psum x1, blocking collectives, shards(): gram_matrix = lax.psum(local_gram, ('outer', 'inner')) / node_count  39.4 us
    all_gather x1, blocking collectives, shards(): z_sep_all = lax.all_gather(z_sep, 'inner', axis=0, tiled=True)  38.3 us
  transfers between devices with their start and end apart: 3, of which 3 were waited for; matrix products, arithmetic and copies ran while one was open for 0% of the time, Pallas kernels for 0%

profile of v1, /device:TPU:0, one launch (start us, length us, event | category | flops | bytes accessed | tf_op | source)
XLA Modules:
  0.0 685.7 jit_solution(16916968704119471954)
XLA Ops:
  7.2 1.4 fusion.17
  8.6 0.4 fusion.18
  9.0 0.7 copy-done.16
  9.7 1.0 fusion.8
  10.8 130.4 %all-reduce.10.cloned.1.call-done = f32[256,64]{1,0:T(8,128)} async-done(((f32[256,64]{1,0:T(8,128)}), f32[256,64]{1,0:T(8,128)}) %all-reduce.10.cloned.1.call-update) | async-done | bytes 65552
  141.3 0.7 dynamic-slice_subtract_fusion
  142.0 40.0 %all_gather.18 = f32[256,64]{1,0:T(8,128)S(1)} all-gather(f32[8,64]{1,0:T(8,128)S(1)} %dynamic-slice_subtract_fusion), channel_id=1, replica_groups=mesh['outer'=1,'inner'=32] {'inner'}, dimensions={0}, use_global_device_ids=true | all-gather | bytes 67584 | tf_op jit(solution)/shard_map/all_gather | solution.py:55
  182.2 0.5 copy-done.11
  182.7 0.9 convolution_bitcast_fusion.3
  183.7 0.6 copy-done.19
  184.3 37.0 %all_gather.19 = f32[256,64]{1,0:T(8,128)S(1)} all-gather(f32[8,64]{1,0:T(8,128)S(1)} %copy-done.18), channel_id=1, replica_groups=mesh['outer'=1,'inner'=32] {'outer','inner'}, dimensions={0}, use_global_device_ids=true | all-gather | bytes 67584 | tf_op jit(solution)/shard_map/all_gather | solution.py:58
  221.4 77.8 %all-reduce.6.cloned.1.call-done = f32[256,64]{0,1:T(8,128)} async-done(((f32[256,64]{0,1:T(8,128)}), f32[256,64]{0,1:T(8,128)}) %all-reduce.6.cloned.1.call-update) | async-done | bytes 65552 | tf_op jit(solution)/shard_map/psum | solution.py:57
  299.2 1.0 convolution_bitcast_fusion.8
  300.2 40.4 %all_gather.20 = f32[256,64]{1,0:T(8,128)S(1)} all-gather(f32[8,64]{1,0:T(8,128)S(1)} %convolution_bitcast_fusion.8), channel_id=1, replica_groups=mesh['outer'=1,'inner'=32] {'outer','inner'}, dimensions={0}, use_global_device_ids=true | all-gather | bytes 67584 | tf_op jit(solution)/shard_map/all_gather | solution.py:60
  340.8 37.0 %all_gather.21 = f32[256,64]{1,0:T(8,128)S(1)} all-gather(f32[8,64]{1,0:T(8,128)S(1)} %bitcast.119), channel_id=1, replica_groups=mesh['outer'=1,'inner'=32] {'outer','inner'}, dimensions={0}, use_global_device_ids=true | all-gather | bytes 67584 | tf_op jit(solution)/shard_map/all_gather | solution.py:62
  377.9 38.3 %all_gather.22 = f32[256,64]{1,0:T(8,128)S(1)} all-gather(f32[8,64]{1,0:T(8,128)S(1)} %fusion.5), channel_id=1, replica_groups=mesh['outer'=1,'inner'=32] {'inner'}, dimensions={0}, use_global_device_ids=true | all-gather | bytes 67584 | tf_op jit(solution)/shard_map/all_gather | solution.py:64
  416.4 37.0 %all_gather.23 = f32[256,64]{1,0:T(8,128)S(1)} all-gather(f32[8,64]{1,0:T(8,128)S(1)} %bitcast.120), channel_id=1, replica_groups=mesh['outer'=1,'inner'=32] {'inner'}, dimensions={0}, use_global_device_ids=true | all-gather | bytes 67584 | tf_op jit(solution)/shard_map/all_gather | solution.py:66
  453.4 0.3 fusion.6
  453.8 0.3 fusion.24
  454.2 0.3 fusion.23
  454.5 0.4 fusion.2
  454.9 0.4 fusion.22
  455.2 1.1 fusion.1
  456.4 122.1 %all-reduce.8.cloned.1.call-done = f32[512,64]{0,1:T(8,128)} async-done(((f32[512,64]{0,1:T(8,128)}), f32[512,64]{0,1:T(8,128)}) %all-reduce.8.cloned.1.call-update) | async-done | bytes 131088 | tf_op jit(solution)/shard_map/psum | solution.py:79
  578.5 0.9 broadcast_multiply_fusion
  579.4 0.6 convolution_subtract_fusion
  580.0 0.2 fusion.4
  580.2 0.2 fusion.3
  580.4 0.2 fusion.25
  580.7 0.2 convolution_add_fusion.2
  580.9 0.2 convolution_add_fusion.1
  581.2 39.4 %psum.40 = f32[64,64]{0,1:T(8,128)S(1)} all-reduce(f32[64,64]{0,1:T(8,128)S(1)} %convolution_add_fusion.1), channel_id=1, replica_groups=mesh['outer'=1,'inner'=32] {'outer','inner'}, use_global_device_ids=true, to_apply=%region_3.0 | all-reduce | flops 4096 | bytes 32768 | tf_op jit(solution)/shard_map/psum | solution.py:88
  620.7 5.8 cholesky.17
  626.6 0.6 compare_reduce_fusion
  627.2 0.7 fusion.13
  627.9 4.9 custom-call.6
  632.8 0.2 fusion.14
  633.0 0.2 fusion.26
  633.3 0.8 fusion.27
  634.0 0.8 fusion.28
  634.8 0.6 gather_fusion
  635.4 0.7 convolution_bitcast_fusion.1
  636.0 0.2 convolution_bitcast_fusion.5
  636.4 0.7 convolution_bitcast_fusion
  637.1 0.2 convolution_bitcast_fusion.4
  637.3 40.4 %all-reduce.1 = (f32[64,64]{0,1:T(8,128)S(1)}, f32[64,64]{0,1:T(8,128)S(1)}) all-reduce(f32[64,64]{0,1:T(8,128)S(1)} %convolution_bitcast_fusion.5, f32[64,64]{0,1:T(8,128)S(1)} %convolution_bitcast_fusion.4), channel_id=1, replica_groups=mesh['outer'=1,'inner'=32] {'outer','inner'}, use_global_device_ids=true, to_apply=%region_6.7 | all-reduce | flops 8192 | bytes 65536 | tf_op jit(solution)/shard_map/psum | solution.py:107
  677.7 0.7 copy.69
  678.4 0.7 copy.70
  (57 shorter events, 1.5 us)
Async XLA Ops:
  7.2 628.2 %copy-start = (f32[1024,128]{1,0:T(8,128)S(1)}, f32[1024,128]{1,0:T(8,128)}, u32[]{:S(2)}) copy-start(f32[1024,128]{1,0:T(8,128)} %param.37) | copy-start | bytes 1572868
  7.2 1.5 copy-start.6
  7.2 134.1 %all-reduce.10.cloned.1.call-start = ((), (), s32[]{:S(2)}) async-start(), calls=%async_computation.2 | async-start | bytes 262144
  9.0 0.7 copy-start.16
  10.8 288.5 %all-reduce.6.cloned.1.call-start = ((), (), s32[]{:S(2)}) async-start(), calls=%async_computation | async-start | bytes 131072 | tf_op jit(solution)/shard_map/psum | solution.py:57
  10.8 130.5 %copy-start.17 = (f32[8,64]{1,0:T(8,128)S(1)}, f32[8,64]{1,0:T(8,128)}, u32[]{:S(2)}) copy-start(f32[8,64]{1,0:T(8,128)} %param.21) | copy-start | bytes 6148
  142.0 40.0 %copy-start.10 = (f32[8,256]{1,0:T(8,128)S(1)}, f32[8,256]{1,0:T(8,128)}, u32[]{:S(2)}) copy-start(f32[8,256]{1,0:T(8,128)} %param.28) | copy-start | bytes 24580
  182.0 0.7 copy-start.11
  183.6 0.7 copy-start.19
  183.6 0.7 copy-start.18
  183.6 394.9 %all-reduce.8.cloned.1.call-start = ((), (), s32[]{:S(2)}) async-start(), calls=%async_computation.1 | async-start | bytes 262144 | tf_op jit(solution)/shard_map/psum | solution.py:79
  221.3 78.0 %copy-start.12 = (f32[8,256]{1,0:T(8,128)S(1)}, f32[8,256]{1,0:T(8,128)}, u32[]{:S(2)}) copy-start(f32[8,256]{1,0:T(8,128)} %param.32) | copy-start | bytes 24580
  300.2 40.4 %copy-start.13 = (f32[8,256]{1,0:T(8,128)S(1)}, f32[8,256]{1,0:T(8,128)}, u32[]{:S(2)}) copy-start(f32[8,256]{1,0:T(8,128)} %param.33) | copy-start | bytes 24580
  340.8 37.0 %copy-start.14 = (f32[8,256]{1,0:T(8,128)S(1)}, f32[8,256]{1,0:T(8,128)}, u32[]{:S(2)}) copy-start(f32[8,256]{1,0:T(8,128)} %param.31) | copy-start | bytes 24580
  377.9 38.3 %copy-start.15 = (f32[8,256]{1,0:T(8,128)S(1)}, f32[8,256]{1,0:T(8,128)}, u32[]{:S(2)}) copy-start(f32[8,256]{1,0:T(8,128)} %param.29) | copy-start | bytes 24580
  416.4 37.3 %copy-start.9 = (f32[8,512]{1,0:T(8,128)S(1)}, f32[8,512]{1,0:T(8,128)}, u32[]{:S(2)}) copy-start(f32[8,512]{1,0:T(8,128)} %param.36) | copy-start | bytes 49156
  453.4 0.7 copy-start.8
  453.4 1.0 copy-start.5
  453.8 1.1 copy-start.7
  454.1 1.1 copy-start.1
  579.4 0.8 copy-start.2
  633.2 3.8 copy-start.3
  635.4 1.0 copy-start.4
Sparse Core Ops, SparseCore 0:
  14.1 127.1 all-reduce.9
  183.7 115.4 all-reduce.5
  456.5 121.9 all-reduce.7
